TPU v7x, 32 devices: a whole 2x2x4 slice. The times are simulated.
32 devices in a mesh: ctx: 8 (over z, x), fsdp: 4 (over y, core).
Axes of the slice: x: 2, y: 2, z: 4, core: 2. Of those that a mesh axis runs over, the one named last changes fastest.
Arguments:
- inputs: bfloat16 [2, 4, 4096, 512], P(None, 'fsdp', 'ctx'), may hold values from -6 to 6
- out_grad: bfloat16 [2, 4, 4096, 512], P(None, 'fsdp', 'ctx'), may hold values from -6 to 6
- segment_ids: int32 [2, 4, 4096], P(None, 'fsdp', 'ctx'), may hold values from 0 to 15, never falling along the last dimension, each value on 1 to 2048 neighbouring positions
- block_order: int32 [16], replicated, may hold values from 0 to 15, each once
- w_qkv: bfloat16 [512, 1536], P('fsdp'), may hold values from -0.25 to 0.25
- w_out: bfloat16 [512, 512], P('fsdp'), may hold values from -1 to 1
- w_up: bfloat16 [512, 2048], P('fsdp'), may hold values from -0.25 to 0.25
- w_down: bfloat16 [2048, 512], P('fsdp'), may hold values from -0.125 to 0.125
- norm1_gain: bfloat16 [512], P('fsdp'), may hold values from 0.25 to 1.75
- norm1_bias: bfloat16 [512], P('fsdp'), may hold values from -2 to 2
- norm2_gain: bfloat16 [512], P('fsdp'), may hold values from 0.25 to 1.75
- norm2_bias: bfloat16 [512], P('fsdp'), may hold values from -2 to 2
- out_bias: bfloat16 [512], P('fsdp'), may hold values from -2 to 2
- up_bias: bfloat16 [2048], P('fsdp'), may hold values from -3 to 3
- down_bias: bfloat16 [512], P('fsdp'), may hold values from -2 to 2
Outputs:
- outputs: bfloat16 [2, 4, 4096, 512], P(None, 'fsdp', 'ctx')
- input_grad: float32 [2, 4, 4096, 512], P(None, 'fsdp', 'ctx')
- grad_w_qkv: float32 [512, 1536], P('fsdp')
- grad_w_out: float32 [512, 512], P('fsdp')
- grad_w_up: float32 [512, 2048], P('fsdp')
- grad_w_down: float32 [2048, 512], P('fsdp')
- grad_norm1_gain: float32 [512], P('fsdp')
- grad_norm1_bias: float32 [512], P('fsdp')
- grad_norm2_gain: float32 [512], P('fsdp')
- grad_norm2_bias: float32 [512], P('fsdp')
- grad_out_bias: float32 [512], P('fsdp')
- grad_up_bias: float32 [2048], P('fsdp')
- grad_down_bias: float32 [512], P('fsdp')
Inputs may be any that keep to these rules, and one draw needn't show every extreme that they name: `segment_ids`: along each sequence's true positions document numbers start at 0 and never fall; each document has 1 to 2048 tokens and one has exactly 2048. `block_order`: each value appears exactly once.
All inputs are finite; a program needn't handle non-finite values.
Results may differ from a plain program's by a relative error of at most 0.02.
Values may be sent and summed in bfloat16 or wider, within the bound.
A program may use at most 256 MiB of HBM per device.

v0:
```python
import math
import jax
import jax.numpy as jnp
from jax import lax
from jax.sharding import PartitionSpec as P

H = 8
HD = 64
BLK = 256
norm_eps = 1e-05
mask_fill = -1e30


def layer_norm(values, gain_vec, offset):
    center = values - jnp.mean(values, axis=-1, keepdims=True)
    spread = jnp.mean(center * center, axis=-1, keepdims=True)
    return center * lax.rsqrt(spread + norm_eps) * gain_vec + offset


def gelu_exact(values):
    return 0.5 * values * (1.0 + lax.erf(values * (1.0 / math.sqrt(2.0))))


def score_block(query_heads, key_heads, query_doc, query_pos, key_doc, key_pos):
    raw_scores = jnp.einsum(
        "qhd,khd->hqk", query_heads, key_heads, preferred_element_type=jnp.float32
    ) * (1.0 / math.sqrt(HD))
    allowed = (query_doc[:, None] == key_doc[None, :]) & (key_pos[None, :] <= query_pos[:, None])
    return (raw_scores, allowed[None])


def soft_block(raw_scores, allowed, log_norm):
    return jnp.exp(jnp.where(allowed, raw_scores, mask_fill) - log_norm[:, :, None])


def row_log_norm(query_heads, key_blocks, doc_blocks, pos_blocks, query_doc, query_pos):

    def row_visit(running, block_item):
        row_top, row_sum = running
        key_heads, key_doc, key_pos = block_item
        raw_scores, allowed = score_block(
            query_heads, key_heads, query_doc, query_pos, key_doc, key_pos
        )
        masked = jnp.where(allowed, raw_scores, mask_fill)
        new_top = jnp.maximum(row_top, jnp.max(masked, axis=-1))
        fresh = jnp.sum(jnp.where(allowed, jnp.exp(masked - new_top[:, :, None]), 0.0), axis=-1)
        return ((new_top, row_sum * jnp.exp(row_top - new_top) + fresh), None)

    query_count = query_doc.shape[0]
    start = (
        jnp.full((H, query_count), mask_fill, jnp.float32),
        jnp.zeros((H, query_count), jnp.float32),
    )
    (row_top, row_sum), unused = lax.scan(row_visit, start, (key_blocks, doc_blocks, pos_blocks))
    return row_top + jnp.log(row_sum)


def attend(
    query_heads, key_blocks, value_blocks, doc_blocks, pos_blocks, query_doc, query_pos, log_norm
):

    def attend_visit(accum_out, block_item):
        key_heads, value_heads, key_doc, key_pos = block_item
        raw_scores, allowed = score_block(
            query_heads, key_heads, query_doc, query_pos, key_doc, key_pos
        )
        soft_low = soft_block(raw_scores, allowed, log_norm).astype(jnp.bfloat16)
        return (
            accum_out
            + jnp.einsum("hqk,khd->qhd", soft_low, value_heads, preferred_element_type=jnp.float32),
            None,
        )

    start = jnp.zeros(query_heads.shape, jnp.float32)
    accum_out, unused = lax.scan(
        attend_visit, start, (key_blocks, value_blocks, doc_blocks, pos_blocks)
    )
    return accum_out


def grad_block(
    query_heads,
    grad_heads,
    log_norm,
    row_delta,
    query_doc,
    query_pos,
    key_heads,
    value_heads,
    key_doc,
    key_pos,
):
    raw_scores, allowed = score_block(
        query_heads, key_heads, query_doc, query_pos, key_doc, key_pos
    )
    soft = soft_block(raw_scores, allowed, log_norm)
    grad_soft = jnp.einsum(
        "qhd,khd->hqk", grad_heads, value_heads, preferred_element_type=jnp.float32
    )
    grad_scores = (soft * (grad_soft - row_delta[:, :, None])).astype(jnp.bfloat16)
    score_scale = 1.0 / math.sqrt(HD)
    part_q = (
        jnp.einsum("hqk,khd->qhd", grad_scores, key_heads, preferred_element_type=jnp.float32)
        * score_scale
    )
    part_k = (
        jnp.einsum("hqk,qhd->khd", grad_scores, query_heads, preferred_element_type=jnp.float32)
        * score_scale
    )
    part_v = jnp.einsum(
        "hqk,qhd->khd", soft.astype(jnp.bfloat16), grad_heads, preferred_element_type=jnp.float32
    )
    return (part_q, part_k, part_v)


def body(
    inputs,
    out_grad,
    segment_ids,
    block_order,
    w_qkv,
    w_out,
    w_up,
    w_down,
    norm1_gain,
    norm1_bias,
    norm2_gain,
    norm2_bias,
    out_bias,
    up_bias,
    down_bias,
):
    gathered = (
        lax.all_gather(w_qkv, "fsdp", axis=0, tiled=True),
        lax.all_gather(w_out, "fsdp", axis=0, tiled=True),
        lax.all_gather(w_up, "fsdp", axis=0, tiled=True),
        lax.all_gather(w_down, "fsdp", axis=0, tiled=True),
        lax.all_gather(norm1_gain, "fsdp", axis=0, tiled=True),
        lax.all_gather(norm1_bias, "fsdp", axis=0, tiled=True),
        lax.all_gather(norm2_gain, "fsdp", axis=0, tiled=True),
        lax.all_gather(norm2_bias, "fsdp", axis=0, tiled=True),
        lax.all_gather(out_bias, "fsdp", axis=0, tiled=True),
        lax.all_gather(up_bias, "fsdp", axis=0, tiled=True),
        lax.all_gather(down_bias, "fsdp", axis=0, tiled=True),
    )
    full_qkv, full_out, full_up, full_down = (gathered[0], gathered[1], gathered[2], gathered[3])
    gain_one, bias_one, gain_two, bias_two, full_obias, full_ubias, full_dbias = [
        member.astype(jnp.float32) for member in gathered[4:]
    ]
    model_width = full_qkv.shape[0]
    local_rows = inputs.shape[2]
    ctx_count = lax.axis_size("ctx")
    seq_len = local_rows * ctx_count
    key_block = min(512, seq_len)
    block_count = seq_len // key_block
    ctx_index = lax.axis_index("ctx")
    row_ids = jnp.arange(local_rows, dtype=jnp.int32)
    own_blocks = lax.dynamic_slice_in_dim(block_order, 2 * ctx_index, 2)
    own_pos = own_blocks[row_ids // BLK] * BLK + row_ids % BLK
    all_ids = jnp.arange(seq_len, dtype=jnp.int32)
    all_pos = block_order[all_ids // BLK] * BLK + all_ids % BLK
    pos_blocks = all_pos.reshape(block_count, key_block)
    grad_sums = [jnp.zeros(member.shape, jnp.float32) for member in gathered]
    outputs_list = []
    input_grads = []
    for micro_idx in range(inputs.shape[0]):
        seq_in = inputs[micro_idx, 0].astype(jnp.float32)
        normed, norm1_pull = jax.vjp(layer_norm, seq_in, gain_one, bias_one)
        normed_low = normed.astype(jnp.bfloat16)
        qkv_out = jnp.dot(normed_low, full_qkv, preferred_element_type=jnp.float32).astype(
            jnp.bfloat16
        )
        query_heads = qkv_out[:, :model_width].reshape(local_rows, H, HD)
        kv_all, doc_all = (
            lax.all_gather(qkv_out[:, model_width:], "ctx", axis=0, tiled=True),
            lax.all_gather(segment_ids[micro_idx, 0], "ctx", axis=0, tiled=True),
        )
        doc_rows = doc_all[all_pos]
        query_doc = doc_all[own_pos]
        kv_heads = kv_all.reshape(block_count, key_block, 2, H, HD)
        key_blocks = kv_heads[:, :, 0]
        value_blocks = kv_heads[:, :, 1]
        doc_blocks = doc_rows.reshape(block_count, key_block)
        log_norm = row_log_norm(query_heads, key_blocks, doc_blocks, pos_blocks, query_doc, own_pos)
        attn_acc = attend(
            query_heads,
            key_blocks,
            value_blocks,
            doc_blocks,
            pos_blocks,
            query_doc,
            own_pos,
            log_norm,
        )
        attn_low = attn_acc.reshape(local_rows, model_width).astype(jnp.bfloat16)
        branch = jnp.dot(attn_low, full_out, preferred_element_type=jnp.float32) + full_obias
        middle = seq_in + branch
        normed_two, norm2_pull = jax.vjp(layer_norm, middle, gain_two, bias_two)
        normed_two_low = normed_two.astype(jnp.bfloat16)
        hidden = jnp.dot(normed_two_low, full_up, preferred_element_type=jnp.float32) + full_ubias
        active, gelu_pull = jax.vjp(gelu_exact, hidden)
        active_low = active.astype(jnp.bfloat16)
        result = middle + (
            jnp.dot(active_low, full_down, preferred_element_type=jnp.float32) + full_dbias
        )
        outputs_list.append(result.astype(jnp.bfloat16))
        grad_y = out_grad[micro_idx, 0]
        grad_y32 = grad_y.astype(jnp.float32)
        grad_sums[3] = grad_sums[3] + jnp.einsum(
            "rf,rd->fd", active_low, grad_y, preferred_element_type=jnp.float32
        )
        grad_sums[10] = grad_sums[10] + jnp.sum(grad_y32, axis=0)
        grad_active = jnp.einsum("rd,fd->rf", grad_y, full_down, preferred_element_type=jnp.float32)
        (grad_hidden,) = gelu_pull(grad_active)
        grad_hidden_low = grad_hidden.astype(jnp.bfloat16)
        grad_sums[2] = grad_sums[2] + jnp.einsum(
            "rd,rf->df", normed_two_low, grad_hidden_low, preferred_element_type=jnp.float32
        )
        grad_sums[9] = grad_sums[9] + jnp.sum(grad_hidden_low.astype(jnp.float32), axis=0)
        grad_normed_two = jnp.einsum(
            "rf,df->rd", grad_hidden_low, full_up, preferred_element_type=jnp.float32
        )
        grad_mid_ln, grad_gain_two, grad_bias_two = norm2_pull(grad_normed_two)
        grad_sums[6] = grad_sums[6] + grad_gain_two
        grad_sums[7] = grad_sums[7] + grad_bias_two
        grad_mid = grad_y32 + grad_mid_ln
        grad_mid_low = grad_mid.astype(jnp.bfloat16)
        grad_sums[1] = grad_sums[1] + jnp.einsum(
            "rd,re->de", attn_low, grad_mid_low, preferred_element_type=jnp.float32
        )
        grad_sums[8] = grad_sums[8] + jnp.sum(grad_mid_low.astype(jnp.float32), axis=0)
        grad_attn_low = jnp.einsum(
            "re,de->rd", grad_mid_low, full_out, preferred_element_type=jnp.float32
        ).astype(jnp.bfloat16)
        grad_heads = grad_attn_low.reshape(local_rows, H, HD)
        row_delta = jnp.sum(grad_heads.astype(jnp.float32) * attn_acc, axis=-1).T

        def back_visit(grad_query, block_item):
            key_heads, value_heads, key_doc, key_pos = block_item
            part_q, part_k, part_v = grad_block(
                query_heads,
                grad_heads,
                log_norm,
                row_delta,
                query_doc,
                own_pos,
                key_heads,
                value_heads,
                key_doc,
                key_pos,
            )
            joined = jnp.concatenate(
                [part_k.reshape(key_block, model_width), part_v.reshape(key_block, model_width)],
                axis=1,
            )
            return (grad_query + part_q, joined)

        grad_query, kv_terms = lax.scan(
            back_visit,
            jnp.zeros((local_rows, H, HD), jnp.float32),
            (key_blocks, value_blocks, doc_blocks, pos_blocks),
        )
        kv_grad = lax.psum_scatter(
            kv_terms.reshape(seq_len, 2 * model_width).astype(jnp.bfloat16),
            "ctx",
            scatter_dimension=0,
            tiled=True,
        ).astype(jnp.float32)
        grad_qkv_low = jnp.concatenate(
            [grad_query.reshape(local_rows, model_width), kv_grad], axis=1
        ).astype(jnp.bfloat16)
        grad_sums[0] = grad_sums[0] + jnp.einsum(
            "rd,re->de", normed_low, grad_qkv_low, preferred_element_type=jnp.float32
        )
        grad_normed = jnp.einsum(
            "re,de->rd", grad_qkv_low, full_qkv, preferred_element_type=jnp.float32
        )
        grad_in_ln, grad_gain_one, grad_bias_one = norm1_pull(grad_normed)
        grad_sums[4] = grad_sums[4] + grad_gain_one
        grad_sums[5] = grad_sums[5] + grad_bias_one
        input_grads.append(grad_mid + grad_in_ln)
    owned = (
        lax.psum_scatter(
            grad_sums[0].astype(jnp.bfloat16), "fsdp", scatter_dimension=0, tiled=True
        ).astype(jnp.float32),
        lax.psum_scatter(
            grad_sums[1].astype(jnp.bfloat16), "fsdp", scatter_dimension=0, tiled=True
        ).astype(jnp.float32),
        lax.psum_scatter(
            grad_sums[2].astype(jnp.bfloat16), "fsdp", scatter_dimension=0, tiled=True
        ).astype(jnp.float32),
        lax.psum_scatter(
            grad_sums[3].astype(jnp.bfloat16), "fsdp", scatter_dimension=0, tiled=True
        ).astype(jnp.float32),
        lax.psum_scatter(
            grad_sums[4].astype(jnp.bfloat16), "fsdp", scatter_dimension=0, tiled=True
        ).astype(jnp.float32),
        lax.psum_scatter(
            grad_sums[5].astype(jnp.bfloat16), "fsdp", scatter_dimension=0, tiled=True
        ).astype(jnp.float32),
        lax.psum_scatter(
            grad_sums[6].astype(jnp.bfloat16), "fsdp", scatter_dimension=0, tiled=True
        ).astype(jnp.float32),
        lax.psum_scatter(
            grad_sums[7].astype(jnp.bfloat16), "fsdp", scatter_dimension=0, tiled=True
        ).astype(jnp.float32),
        lax.psum_scatter(
            grad_sums[8].astype(jnp.bfloat16), "fsdp", scatter_dimension=0, tiled=True
        ).astype(jnp.float32),
        lax.psum_scatter(
            grad_sums[9].astype(jnp.bfloat16), "fsdp", scatter_dimension=0, tiled=True
        ).astype(jnp.float32),
        lax.psum_scatter(
            grad_sums[10].astype(jnp.bfloat16), "fsdp", scatter_dimension=0, tiled=True
        ).astype(jnp.float32),
    )
    summed = (
        lax.psum(owned[0].astype(jnp.bfloat16), "ctx").astype(jnp.float32),
        lax.psum(owned[1].astype(jnp.bfloat16), "ctx").astype(jnp.float32),
        lax.psum(owned[2].astype(jnp.bfloat16), "ctx").astype(jnp.float32),
        lax.psum(owned[3].astype(jnp.bfloat16), "ctx").astype(jnp.float32),
        lax.psum(owned[4].astype(jnp.bfloat16), "ctx").astype(jnp.float32),
        lax.psum(owned[5].astype(jnp.bfloat16), "ctx").astype(jnp.float32),
        lax.psum(owned[6].astype(jnp.bfloat16), "ctx").astype(jnp.float32),
        lax.psum(owned[7].astype(jnp.bfloat16), "ctx").astype(jnp.float32),
        lax.psum(owned[8].astype(jnp.bfloat16), "ctx").astype(jnp.float32),
        lax.psum(owned[9].astype(jnp.bfloat16), "ctx").astype(jnp.float32),
        lax.psum(owned[10].astype(jnp.bfloat16), "ctx").astype(jnp.float32),
    )
    return (
        jnp.stack(outputs_list)[:, None],
        jnp.stack(input_grads)[:, None],
        summed[0],
        summed[1],
        summed[2],
        summed[3],
        summed[4],
        summed[5],
        summed[6],
        summed[7],
        summed[8],
        summed[9],
        summed[10],
    )


def solution(mesh):
    return jax.shard_map(
        body,
        mesh=mesh,
        in_specs=(
            P(None, "fsdp", "ctx", None),
            P(None, "fsdp", "ctx", None),
            P(None, "fsdp", "ctx"),
            P(),
            P("fsdp", None),
            P("fsdp", None),
            P("fsdp", None),
            P("fsdp", None),
            P("fsdp"),
            P("fsdp"),
            P("fsdp"),
            P("fsdp"),
            P("fsdp"),
            P("fsdp"),
            P("fsdp"),
        ),
        out_specs=(
            P(None, "fsdp", "ctx", None),
            P(None, "fsdp", "ctx", None),
            P("fsdp", None),
            P("fsdp", None),
            P("fsdp", None),
            P("fsdp", None),
            P("fsdp"),
            P("fsdp"),
            P("fsdp"),
            P("fsdp"),
            P("fsdp"),
            P("fsdp"),
            P("fsdp"),
        ),
        check_vma=False,
    )
```

profile of v0, /device:TPU:0, one launch (start us, length us, event | category | flops | bytes accessed | tf_op | source)
XLA Modules:
  0.0 1195.3 jit_solution(4293471570105327463)
XLA Ops:
  21.4 10.5 all-gather.15.cloned.1.call-done
  45.4 27.0 %all-gather = s32[1,1,4096]{2,1,0:T(1,128)S(1)} all-gather(s32[1,1,512]{2,1,0:T(1,128)S(1)} %get-tuple-element.1148), channel_id=2, replica_groups=mesh['ctx'=8,'fsdp'=4] {'ctx'}, dimensions={2}, use_global_device_ids=true | all-gather | bytes 18432 | tf_op jit(solution)/shard_map/all_gather | solution.py:176
  85.7 23.0 %gather_fusion.1 = s32[4096]{0:T(1024)S(1)} fusion(s32[4096]{0:T(1024)S(1)} %bitcast.527, s32[4096]{0:T(1024)S(1)} %broadcast_clamp_fusion), kind=kCustom, calls=%fused_computation.1 | custom fusion | bytes 49152 | tf_op jit(solution)/shard_map/gather | solution.py:178
  108.7 26.7 %all-gather.1 = s32[1,1,4096]{2,1,0:T(1,128)S(1)} all-gather(s32[1,1,512]{2,1,0:T(1,128)S(1)} %get-tuple-element.1149), channel_id=3, replica_groups=mesh['ctx'=8,'fsdp'=4] {'ctx'}, dimensions={2}, use_global_device_ids=true | all-gather | bytes 18432 | tf_op jit(solution)/shard_map/all_gather | solution.py:176
  138.6 23.0 %gather_fusion.3 = s32[4096]{0:T(1024)S(1)} fusion(s32[4096]{0:T(1024)S(1)} %bitcast.529, s32[4096]{0:T(1024)S(1)} %broadcast_clamp_fusion), kind=kCustom, calls=%fused_computation.3 | custom fusion | bytes 49152 | tf_op jit(solution)/shard_map/gather | solution.py:178
  182.3 7.2 all_gather.50
  195.1 11.4 copy.162
  206.6 12.2 %copy.239 = bf16[128,8,8,512]{3,2,1,0:T(8,128)(2,1)} copy(bf16[128,8,8,512]{3,1,2,0:T(8,128)(2,1)} %bitcast.538) | data formatting | bytes 16777216
  227.5 50.1 %while.76 = (s32[]{:T(128)}, f32[8,512]{1,0:T(8,128)S(1)}, f32[8,512]{1,0:T(8,128)S(1)}, s32[512]{0:T(512)S(1)}, s32[8,512]{1,0:T(8,128)S(1)}, /*index=5*/s32[8,...) while((s32[]{:T(128)}, f32[8,512]{1,0:T(8,128)S(1)}, ...), condition=%wide.region_15.16_spmd.clone, body=%wide.region_12.15_spmd.clone.sunk | while | flops 286030336 | bytes 18847896 | solution.py:54
  277.6 10.2 all-gather.17.cloned.1.call-done
  287.8 11.7 copy.155
  299.6 12.2 %copy.238 = bf16[128,8,8,512]{3,2,1,0:T(8,128)(2,1)} copy(bf16[128,8,8,512]{3,1,2,0:T(8,128)(2,1)} %bitcast.539) | data formatting | bytes 16777216
  320.5 50.5 %while.74 = (s32[]{:T(128)}, f32[8,512]{1,0:T(8,128)S(1)}, f32[8,512]{1,0:T(8,128)S(1)}, s32[512]{0:T(512)S(1)}, s32[8,512]{1,0:T(8,128)S(1)}, /*index=5*/s32[8,...) while((s32[]{:T(128)}, f32[8,512]{1,0:T(8,128)S(1)}, ...), condition=%wide.region_5.6_spmd.clone, body=%wide.region_2.5_spmd.clone.sunk | while | flops 286030336 | bytes 18847896 | solution.py:54
  377.3 46.4 %while.75 = (s32[]{:T(128)}, f32[512,8,64]{0,2,1:T(8,128)S(1)}, bf16[8,512,8,64]{1,3,2,0:T(8,128)(2,1)}, s32[512]{0:T(512)S(1)}, s32[8,512]{1,0:T(8,128)S(1)}, /...) while((s32[]{:T(128)}, f32[512,8,64]{0,2,1:T(8,128)S(1)}, ...), condition=%wide.region_7.8_spmd.clone, body=%wide.region_6.7_spmd.clone.sunk | while | flops 546580992 | bytes 4234906 | solution.py:75
  430.4 46.4 %while.77 = (s32[]{:T(128)}, f32[512,8,64]{0,2,1:T(8,128)S(1)}, bf16[8,512,8,64]{1,3,2,0:T(8,128)(2,1)}, s32[512]{0:T(512)S(1)}, s32[8,512]{1,0:T(8,128)S(1)}, /...) while((s32[]{:T(128)}, f32[512,8,64]{0,2,1:T(8,128)S(1)}, ...), condition=%wide.region_17.18_spmd.clone, body=%wide.region_16.17_spmd.clone.sunk | while | flops 546580992 | bytes 4234906 | solution.py:75
  525.5 138.9 %while.78 = (s32[]{:T(128)}, f32[512,8,64]{0,2,1:T(8,128)}, bf16[8,512,1024]{2,1,0:T(8,128)(2,1)}, bf16[8,512,8,64]{1,3,2,0:T(8,128)(2,1)}, s32[512]{0:T(512)S(1...) while((s32[]{:T(128)}, f32[512,8,64]{0,2,1:T(8,128)}, ...), condition=%wide.region_24.25_spmd.clone, body=%wide.region_23.24_spmd.clone.sunk | while | flops 1367353856 | bytes 51714240 | solution.py:258
  668.7 131.5 %while.79 = (s32[]{:T(128)}, f32[512,8,64]{0,2,1:T(8,128)}, bf16[8,512,1024]{2,1,0:T(8,128)(2,1)}, bf16[8,512,8,64]{1,3,2,0:T(8,128)(2,1)}, s32[512]{0:T(512)S(1...) while((s32[]{:T(128)}, f32[512,8,64]{0,2,1:T(8,128)}, ...), condition=%wide.region_32.33_spmd.clone, body=%wide.region_31.32_spmd.clone.sunk | while | flops 1367353856 | bytes 51714240 | solution.py:258
  834.8 129.0 %reduce-scatter.9.cloned.1.call-done = bf16[512,1024]{1,0:T(8,128)(2,1)} async-done(((bf16[4096,1024]{1,0:T(8,128)(2,1)}), bf16[512,1024]{1,0:T(8,128)(2,1)}) %reduce-scatter.9.cloned.1.call-update) | async-done | bytes 1048592 | tf_op jit(solution)/shard_map/reduce_scatter | solution.py:263
  987.0 34.2 %reduce-scatter.15.cloned.1.call-done = bf16[128,2048]{1,0:T(8,128)(2,1)} async-done(((bf16[512,2048]{1,0:T(8,128)(2,1)}), bf16[128,2048]{1,0:T(8,128)(2,1)}) %reduce-scatter.15.cloned.1.call-update) | async-done | bytes 524304 | tf_op jit(solution)/shard_map/reduce_scatter | solution.py:289
  1021.1 33.9 %reduce-scatter.17.cloned.1.call-done = bf16[512,512]{1,0:T(8,128)(2,1)} async-done(((bf16[2048,512]{1,0:T(8,128)(2,1)}), bf16[512,512]{1,0:T(8,128)(2,1)}) %reduce-scatter.17.cloned.1.call-update) | async-done | bytes 524304 | tf_op jit(solution)/shard_map/reduce_scatter | solution.py:292
  1055.0 31.5 %reduce-scatter.11.cloned.1.call-done = bf16[128,1536]{1,0:T(8,128)(2,1)} async-done(((bf16[512,1536]{1,0:T(8,128)(2,1)}), bf16[128,1536]{1,0:T(8,128)(2,1)}) %reduce-scatter.11.cloned.1.call-update) | async-done | bytes 393232 | tf_op jit(solution)/shard_map/reduce_scatter | solution.py:283
  1091.7 10.5 all-reduce.9
  1102.8 22.1 %all-reduce.7 = (bf16[128]{0:T(256)(128)(2,1)S(1)}, bf16[128]{0:T(256)(128)(2,1)S(1)}, bf16[128]{0:T(256)(128)(2,1)S(1)}, bf16[128]{0:T(256)(128)(2,1)S(1)}, bf1...) all-reduce(bf16[128]{0:T(256)(128)(2,1)S(1)} %dynamic-slice.1, ...), channel_id=1, replica_groups=mesh['ctx'=8,'fsdp'=4] {'ctx'}, use_global_device_ids=true, to_apply=%region_47.48 | all-reduce | flops 1280 | bytes 5120 | tf_op jit(solution)/shard_map/psum | solution.py:322
  1131.7 48.7 %all-reduce.12.cloned.1.call-done = (bf16[128,1536]{1,0:T(8,128)(2,1)}, bf16[128,512]{1,0:T(8,128)(2,1)}, bf16[128,2048]{1,0:T(8,128)(2,1)}, bf16[512,512]{1,0:T(8,128)(2,1)}) async-done(((bf16[128,1536]{1,0:T(8,128)(2,1)}, bf16[128,512]{1,0:T(8,128)(2,1)}, bf16[128,2048]{1,0:T(8,128)(2,1)}, bf16[512,512]{1,0:T(8,128)(2,1)}), (bf16[128,1536]{1,0:T(8,128)(2,1)}, bf16[128,512]{1,0:T(8,128)(2,1)}, ...) | async-done | bytes 1572880 | tf_op jit(solution)/shard_map/psum | solution.py:318
  (807 shorter events, 689.0 us)
Async XLA Ops:
  7.2 24.8 %all-gather.15.cloned.1.call-start = ((), (), s32[]{:S(2)}) async-start(), calls=%async_computation.6 | async-start | bytes 1966080 | tf_op jit(solution)/shard_map/all_gather | solution.py:134
  7.9 187.2 %all-gather.23.cloned.1.call-start = ((), (), s32[]{:S(2)}) async-start(), calls=%async_computation.10 | async-start | bytes 9437184 | tf_op jit(solution)/shard_map/all_gather | solution.py:175
  36.8 251.0 %all-gather.17.cloned.1.call-start = ((), (), s32[]{:S(2)}) async-start(), calls=%async_computation.7 | async-start | bytes 9437184 | tf_op jit(solution)/shard_map/all_gather | solution.py:175
  37.1 441.5 %copy-start.7 = (bf16[1,1,512,512]{2,3,1,0:T(8,128)(2,1)}, bf16[1,1,512,512]{2,3,1,0:T(8,128)(2,1)S(1)}, u32[]{:S(2)}) copy-start(bf16[1,1,512,512]{2,3,1,0:T(8,128)(2,1)S(1)} %copy.202) | copy-start | bytes 1572868
  40.9 440.4 %all-gather.19.cloned.1.call-start = ((), (), s32[]{:S(2)}) async-start(), calls=%async_computation.8 | async-start | bytes 2621440 | tf_op jit(solution)/shard_map/all_gather | solution.py:136
  41.5 444.9 %all-gather.21.cloned.1.call-start = ((), (), s32[]{:S(2)}) async-start(), calls=%async_computation.9 | async-start | bytes 2621440 | tf_op jit(solution)/shard_map/all_gather | solution.py:137
  42.1 788.4 %reduce-scatter.7.cloned.1.call-start = ((), (), s32[]{:S(2)}) async-start(), calls=%async_computation.11 | async-start | bytes 9437184 | tf_op jit(solution)/shard_map/reduce_scatter | solution.py:263
  138.6 50.9 %copy-start.28 = (bf16[2,1,512,512]{3,2,1,0:T(8,128)(2,1)S(1)}, bf16[2,1,512,512]{3,2,1,0:T(8,128)(2,1)}, u32[]{:S(2)}) copy-start(bf16[2,1,512,512]{3,2,1,0:T(8,128)(2,1)} %param.28) | copy-start | bytes 3145732
  167.0 349.0 %copy-start.47 = (f32[4,1,128]{2,1,0:T(1,128)}, f32[4,1,128]{2,1,0:T(1,128)S(1)}, u32[]{:S(2)}) copy-start(f32[4,1,128]{2,1,0:T(1,128)S(1)} %convert_element_type.307) | copy-start | bytes 6148
  172.0 325.7 %copy-start.53 = (f32[4,1,128]{2,1,0:T(1,128)}, f32[4,1,128]{2,1,0:T(1,128)S(1)}, u32[]{:S(2)}) copy-start(f32[4,1,128]{2,1,0:T(1,128)S(1)} %convert_element_type.308) | copy-start | bytes 6148
  189.5 289.0 %copy-start.9 = (bf16[512,512]{1,0:T(8,128)(2,1)}, bf16[512,512]{1,0:T(8,128)(2,1)S(1)}, u32[]{:S(2)}) copy-start(bf16[512,512]{1,0:T(8,128)(2,1)S(1)} %all_gather.50) | copy-start | bytes 1572868
  664.4 299.4 %reduce-scatter.9.cloned.1.call-start = ((), (), s32[]{:S(2)}) async-start(), calls=%async_computation.12 | async-start | bytes 9437184 | tf_op jit(solution)/shard_map/reduce_scatter | solution.py:263
  800.3 186.7 %reduce-scatter.13.cloned.1.call-start = ((), (), s32[]{:S(2)}) async-start(), calls=%async_computation.14 | async-start | bytes 655360 | tf_op jit(solution)/shard_map/reduce_scatter | solution.py:286
  803.2 218.0 %reduce-scatter.15.cloned.1.call-start = ((), (), s32[]{:S(2)}) async-start(), calls=%async_computation.15 | async-start | bytes 2621440 | tf_op jit(solution)/shard_map/reduce_scatter | solution.py:289
  809.2 245.8 %reduce-scatter.17.cloned.1.call-start = ((), (), s32[]{:S(2)}) async-start(), calls=%async_computation.16 | async-start | bytes 2621440 | tf_op jit(solution)/shard_map/reduce_scatter | solution.py:292
  815.1 271.4 %reduce-scatter.11.cloned.1.call-start = ((), (), s32[]{:S(2)}) async-start(), calls=%async_computation.13 | async-start | bytes 1966080 | tf_op jit(solution)/shard_map/reduce_scatter | solution.py:283
  830.5 133.3 %copy-start.6 = (bf16[1,1,512,512]{2,3,1,0:T(8,128)(2,1)S(1)}, bf16[1,1,512,512]{2,3,1,0:T(8,128)(2,1)}, u32[]{:S(2)}) copy-start(bf16[1,1,512,512]{2,3,1,0:T(8,128)(2,1)} %copy-done.4) | copy-start | bytes 1572868
  830.5 133.3 %copy-start.62 = (f32[512]{0:T(512)S(1)}, f32[512]{0:T(512)}, u32[]{:S(2)}) copy-start(f32[512]{0:T(512)} %copy-done.61) | copy-start | bytes 6148
  830.5 133.3 %copy-start.68 = (f32[512]{0:T(512)S(1)}, f32[512]{0:T(512)}, u32[]{:S(2)}) copy-start(f32[512]{0:T(512)} %copy-done.67) | copy-start | bytes 6148
  968.2 212.2 %all-reduce.12.cloned.1.call-start = ((), (), s32[]{:S(2)}) async-start(), calls=%async_computation.17 | async-start | bytes 3145728 | tf_op jit(solution)/shard_map/psum | solution.py:318
  981.3 105.2 %copy-start.27 = (bf16[1,1,512,512]{2,3,1,0:T(8,128)(2,1)S(1)}, bf16[1,1,512,512]{2,3,1,0:T(8,128)(2,1)}, u32[]{:S(2)}) copy-start(bf16[1,1,512,512]{2,3,1,0:T(8,128)(2,1)} %copy.204) | copy-start | bytes 1572868
  981.3 105.2 %copy-start.78 = (f32[512]{0:T(512)S(1)}, f32[512]{0:T(512)}, u32[]{:S(2)}) copy-start(f32[512]{0:T(512)} %copy-done.77) | copy-start | bytes 6148
  986.3 103.6 %copy-start.23 = (bf16[1,1,512,512]{2,3,1,0:T(8,128)(2,1)S(1)}, bf16[1,1,512,512]{2,3,1,0:T(8,128)(2,1)}, u32[]{:S(2)}) copy-start(bf16[1,1,512,512]{2,3,1,0:T(8,128)(2,1)} %copy.205) | copy-start | bytes 1572868
  986.3 103.6 %copy-start.76 = (f32[512]{0:T(512)S(1)}, f32[512]{0:T(512)}, u32[]{:S(2)}) copy-start(f32[512]{0:T(512)} %copy-done.75) | copy-start | bytes 6148
  (88 other events, 731.3 us)
Sparse Core Ops, SparseCore 0:
  9.6 22.3 all-gather.14
  36.9 125.5 all-gather.22
  164.7 123.0 all-gather.16
  289.2 20.7 all-gather.18
  311.5 22.5 all-gather.20
  664.5 147.1 reduce-scatter.6
  815.8 147.9 reduce-scatter.8
  966.3 20.6 reduce-scatter.12
  989.7 31.4 reduce-scatter.14
  1023.5 31.4 reduce-scatter.16
  1058.3 28.1 reduce-scatter.10
  1090.2 90.2 all-reduce.11
where the time goes:
time: 1210 us; the launch traced here: 1200 us
  matrix products  395 us (33%)
  waiting for transfers between devices  301 us (25%)
  local copies, waits for them, and re-layouts  193 us (16%)
  other arithmetic  155 us (13%)
  blocking collectives  131 us (11%)
  between operations  17.2 us (1%)
    reduce_scatter x2, waiting for transfers between devices, body(): lax.psum_scatter(kv_terms.reshape(seq_len, 2 * model_width).astype(jnp.bf...  129 us
    dot_general x32, matrix products, score_block(): jnp.einsum('qhd,khd->hqk', query_heads, key_heads, preferred_element_type...  77.9 us
    dot_general x16, matrix products, attend_visit(): jnp.einsum('hqk,khd->qhd', soft_low, value_heads, preferred_element_type=...  66.4 us
    dot_general x16, matrix products, grad_block(): jnp.einsum('qhd,khd->hqk', grad_heads, value_heads, preferred_element_typ...  64.5 us
    mul x48, other arithmetic, body(): own_pos = own_blocks[row_ids // BLK] * BLK + row_ids % BLK  62.6 us
    unnamed x219, local copies, waits for them, and re-layouts  55.3 us
    all_gather x2, blocking collectives, body(): lax.all_gather(segment_ids[micro_idx, 0], 'ctx', axis=0, tiled=True)  53.6 us
    dot_general x16, matrix products, grad_block(): jnp.einsum('hqk,khd->qhd', grad_scores, key_heads, preferred_element_type...  50 us
  transfers between devices with their start and end apart: 12, of which 8 were waited for; matrix products, arithmetic and copies ran while one was open for 46% of the time, Pallas kernels for 0%

commit v1 on v0

--- a/solution.py
+++ b/solution.py
@@ -9,6 +9,19 @@
 BLK = 256
 norm_eps = 1e-05
 mask_fill = -1e30
+
+
+def ring_gather(shard, axis, dim):
+    ways = lax.axis_size(axis)
+    up = [(d, (d + 1) % ways) for d in range(ways)]
+    down = [(d, (d - 1) % ways) for d in range(ways)]
+    earlier, later = ([shard], [shard])
+    for _ in range(ways // 2):
+        earlier.append(lax.ppermute(earlier[-1], axis, up))
+    for _ in range((ways - 1) // 2):
+        later.append(lax.ppermute(later[-1], axis, down))
+    line = jnp.concatenate([*earlier[::-1], *later[1:]], axis=dim)
+    return jnp.roll(line, (lax.axis_index(axis) - ways // 2) * shard.shape[dim], axis=dim)
 
 
 def layer_norm(values, gain_vec, offset):
@@ -172,7 +185,7 @@
         )
         query_heads = qkv_out[:, :model_width].reshape(local_rows, H, HD)
         kv_all, doc_all = (
-            lax.all_gather(qkv_out[:, model_width:], "ctx", axis=0, tiled=True),
+            ring_gather(qkv_out[:, model_width:], "ctx", 0),
             lax.all_gather(segment_ids[micro_idx, 0], "ctx", axis=0, tiled=True),
         )
         doc_rows = doc_all[all_pos]

time: 1210 us -> 1530 us (1.26)
  waiting for transfers between devices: 301 us -> 515 us
  blocking collectives: 131 us -> 166 us
  starting transfers between devices: 0.49 us -> 23.7 us
  local copies, waits for them, and re-layouts: 193 us -> 213 us
  other arithmetic: 155 us -> 172 us
    ppermute x0 -> x14, waiting for transfers between devices: none -> 230 us  [the longest x8 188 us: ring_gather(): earlier.append(lax.ppermute(earlier[-1], axis, up))]
    all_gather x2, blocking collectives: 53.6 us -> 89.3 us  [body(): lax.all_gather(segment_ids[micro_idx, 0], 'ctx', axis=0, tiled=True)]
    all_gather x2 -> x0, local copies, waits for them, and re-layouts: 23.2 us -> none  [body(): lax.all_gather(qkv_out[:, model_width:], 'ctx', axis=0, tiled=True)]
    dynamic_slice x0 -> x2, local copies, waits for them, and re-layouts: none -> 22.6 us  [ring_gather(): jnp.roll(line, (lax.axis_index(axis) - ways // 2) * shard.shape[dim], axi...]
    ppermute x0 -> x14, starting transfers between devices: none -> 22.5 us  [the longest x8 13.2 us: ring_gather(): earlier.append(lax.ppermute(earlier[-1], axis, up))]
    concatenate x0 -> x1, other arithmetic: none -> 17.8 us  [ring_gather(): jnp.roll(line, (lax.axis_index(axis) - ways // 2) * shard.shape[dim], axi...]
    unnamed x219 -> x247, local copies, waits for them, and re-layouts: 55.3 us -> 68.4 us
  transfers between devices with their start and end apart: 12 -> 24, of which waited for: 8 -> 13; matrix products, arithmetic and copies ran while one was open for 46% -> 31% of each run, Pallas kernels for 0% -> 0%
where the time goes in v1:
time: 1530 us; the launch traced here: 1510 us
  waiting for transfers between devices  515 us (34%)
  matrix products  403 us (26%)
  local copies, waits for them, and re-layouts  213 us (14%)
  other arithmetic  172 us (11%)
  blocking collectives  166 us (11%)
  starting transfers between devices  23.7 us (2%)
  between operations  17.4 us (1%)
    ppermute x8, waiting for transfers between devices, ring_gather(): earlier.append(lax.ppermute(earlier[-1], axis, up))  188 us
    reduce_scatter x2, waiting for transfers between devices, body(): lax.psum_scatter(kv_terms.reshape(seq_len, 2 * model_width).astype(jnp.bf...  125 us
    all_gather x2, blocking collectives, body(): lax.all_gather(segment_ids[micro_idx, 0], 'ctx', axis=0, tiled=True)  89.3 us
    dot_general x32, matrix products, score_block(): jnp.einsum('qhd,khd->hqk', query_heads, key_heads, preferred_element_type...  78 us
    dot_general x16, matrix products, attend_visit(): jnp.einsum('hqk,khd->qhd', soft_low, value_heads, preferred_element_type=...  75.7 us
    unnamed x247, local copies, waits for them, and re-layouts  68.4 us
    dot_general x16, matrix products, grad_block(): jnp.einsum('qhd,khd->hqk', grad_heads, value_heads, preferred_element_typ...  64.4 us
    mul x48, other arithmetic, body(): own_pos = own_blocks[row_ids // BLK] * BLK + row_ids % BLK  62.6 us
  transfers between devices with their start and end apart: 24, of which 13 were waited for; matrix products, arithmetic and copies ran while one was open for 31% of the time, Pallas kernels for 0%

profile of v1, /device:TPU:0, one launch (start us, length us, event | category | flops | bytes accessed | tf_op | source)
XLA Modules:
  0.0 1512.1 jit_solution(11973192845284260576)
XLA Ops:
  41.2 22.4 %collective-permute-done = bf16[512,1024]{1,0:T(8,128)(2,1)} collective-permute-done((bf16[512,1024]{1,0:T(8,128)(2,1)S(1)}, bf16[512,1024]{1,0:T(8,128)(2,1)}, u32[]{:S(2)}, u32[]{:S(2)}) %collective-permute-start) | collective-permute-done | bytes 1048608 | tf_op jit(solution)/shard_map/ppermute | solution.py:20
  80.0 47.4 %collective-permute-done.7 = bf16[512,1024]{1,0:T(8,128)(2,1)} collective-permute-done((bf16[512,1024]{1,0:T(8,128)(2,1)}, bf16[512,1024]{1,0:T(8,128)(2,1)}, u32[]{:S(2)}, u32[]{:S(2)}) %collective-permute-start.7) | collective-permute-done | bytes 1048608 | tf_op jit(solution)/shard_map/ppermute | solution.py:20
  129.8 20.0 %collective-permute-done.1 = bf16[512,1024]{1,0:T(8,128)(2,1)} collective-permute-done((bf16[512,1024]{1,0:T(8,128)(2,1)}, bf16[512,1024]{1,0:T(8,128)(2,1)}, u32[]{:S(2)}, u32[]{:S(2)}) %collective-permute-start.1) | collective-permute-done | bytes 1048608 | tf_op jit(solution)/shard_map/ppermute | solution.py:20
  155.9 42.0 %collective-permute-done.4 = bf16[512,1024]{1,0:T(8,128)(2,1)} collective-permute-done((bf16[512,1024]{1,0:T(8,128)(2,1)}, bf16[512,1024]{1,0:T(8,128)(2,1)}, u32[]{:S(2)}, u32[]{:S(2)}) %collective-permute-start.4) | collective-permute-done | bytes 1048608 | tf_op jit(solution)/shard_map/ppermute | solution.py:22
  199.9 39.8 %collective-permute-done.2 = bf16[512,1024]{1,0:T(8,128)(2,1)} collective-permute-done((bf16[512,1024]{1,0:T(8,128)(2,1)}, bf16[512,1024]{1,0:T(8,128)(2,1)}, u32[]{:S(2)}, u32[]{:S(2)}) %collective-permute-start.2) | collective-permute-done | bytes 1048608 | tf_op jit(solution)/shard_map/ppermute | solution.py:20
  243.5 63.3 %all-gather = s32[1,1,4096]{2,1,0:T(1,128)S(1)} all-gather(s32[1,1,512]{2,1,0:T(1,128)S(1)} %get-tuple-element.1149), channel_id=2, replica_groups=mesh['ctx'=8,'fsdp'=4] {'ctx'}, dimensions={2}, use_global_device_ids=true | all-gather | bytes 18432 | tf_op jit(solution)/shard_map/all_gather | solution.py:189
  310.0 23.0 %gather_fusion.1 = s32[4096]{0:T(1024)S(1)} fusion(s32[4096]{0:T(1024)S(1)} %bitcast.527, s32[4096]{0:T(1024)S(1)} %broadcast_clamp_fusion), kind=kCustom, calls=%fused_computation.1 | custom fusion | bytes 49152 | tf_op jit(solution)/shard_map/gather | solution.py:191
  333.0 26.0 %all-gather.1 = s32[1,1,4096]{2,1,0:T(1,128)S(1)} all-gather(s32[1,1,512]{2,1,0:T(1,128)S(1)} %get-tuple-element.1150), channel_id=3, replica_groups=mesh['ctx'=8,'fsdp'=4] {'ctx'}, dimensions={2}, use_global_device_ids=true | all-gather | bytes 18432 | tf_op jit(solution)/shard_map/all_gather | solution.py:189
  362.2 23.0 %gather_fusion.3 = s32[4096]{0:T(1024)S(1)} fusion(s32[4096]{0:T(1024)S(1)} %bitcast.529, s32[4096]{0:T(1024)S(1)} %broadcast_clamp_fusion), kind=kCustom, calls=%fused_computation.3 | custom fusion | bytes 49152 | tf_op jit(solution)/shard_map/gather | solution.py:191
  431.9 57.9 %collective-permute-done.10 = bf16[512,1024]{1,0:T(8,128)(2,1)S(1)} collective-permute-done((bf16[512,1024]{1,0:T(8,128)(2,1)}, bf16[512,1024]{1,0:T(8,128)(2,1)S(1)}, u32[]{:S(2)}, u32[]{:S(2)}) %collective-permute-start.10) | collective-permute-done | bytes 1048608 | tf_op jit(solution)/shard_map/ppermute | solution.py:20
  496.7 17.8 %fusion.144 = (bf16[4096,1024]{1,0:T(8,128)(2,1)}, bf16[4096,1024]{1,0:T(8,128)(2,1)}) fusion(s32[]{:T(128)S(6)} %select_n.277, bf16[4096,1024]{1,0:T(8,128)(2,1)S(1)} %constant_dynamic-update-slice_fusion.10, bf16[4096,1024]{1,0:T(8,128)(2,1)S(1)} %constant_dynamic-update-slice_fusion.2), kind=kLoop, calls=%fused_computation.214 | loop fusion | flops 33554432 | bytes 33554436 | tf_op jit(solution)/shard_map/jit(_roll_dynamic)/concatenate | solution.py:24
  547.0 50.1 %while.76 = (s32[]{:T(128)}, f32[8,512]{1,0:T(8,128)S(1)}, f32[8,512]{1,0:T(8,128)S(1)}, s32[512]{0:T(512)S(1)}, s32[8,512]{1,0:T(8,128)S(1)}, /*index=5*/s32[8,...) while((s32[]{:T(128)}, f32[8,512]{1,0:T(8,128)S(1)}, ...), condition=%wide.region_15.17_spmd.clone, body=%wide.region_12.16_spmd.clone.sunk | while | flops 286030336 | bytes 18847896 | solution.py:67
  602.6 55.3 %while.77 = (s32[]{:T(128)}, f32[512,8,64]{0,2,1:T(8,128)}, bf16[8,512,8,64]{1,3,2,0:T(8,128)(2,1)}, s32[512]{0:T(512)S(1)}, s32[8,512]{1,0:T(8,128)S(1)}, /*ind...) while((s32[]{:T(128)}, f32[512,8,64]{0,2,1:T(8,128)}, ...), condition=%wide.region_17.19_spmd.clone, body=%wide.region_16.18_spmd.clone.sunk | while | flops 546580992 | bytes 4234906 | solution.py:88
  686.9 12.2 copy.234
  707.9 50.3 %while.74 = (s32[]{:T(128)}, f32[8,512]{1,0:T(8,128)S(1)}, f32[8,512]{1,0:T(8,128)S(1)}, s32[512]{0:T(512)S(1)}, s32[8,512]{1,0:T(8,128)S(1)}, /*index=5*/s32[8,...) while((s32[]{:T(128)}, f32[8,512]{1,0:T(8,128)S(1)}, ...), condition=%wide.region_5.7_spmd.clone, body=%wide.region_2.6_spmd.clone.sunk | while | flops 286030336 | bytes 18847896 | solution.py:67
  763.9 46.6 %while.75 = (s32[]{:T(128)}, f32[512,8,64]{0,2,1:T(8,128)S(1)}, bf16[8,512,8,64]{1,3,2,0:T(8,128)(2,1)}, s32[512]{0:T(512)S(1)}, s32[8,512]{1,0:T(8,128)S(1)}, /...) while((s32[]{:T(128)}, f32[512,8,64]{0,2,1:T(8,128)S(1)}, ...), condition=%wide.region_7.9_spmd.clone, body=%wide.region_6.8_spmd.clone.sunk | while | flops 546580992 | bytes 4234906 | solution.py:88
  840.4 138.7 %while.78 = (s32[]{:T(128)}, f32[512,8,64]{0,2,1:T(8,128)}, bf16[8,512,1024]{2,1,0:T(8,128)(2,1)}, bf16[8,512,8,64]{1,3,2,0:T(8,128)(2,1)}, s32[512]{0:T(512)S(1...) while((s32[]{:T(128)}, f32[512,8,64]{0,2,1:T(8,128)}, ...), condition=%wide.region_24.26_spmd.clone, body=%wide.region_23.25_spmd.clone.sunk | while | flops 1367353856 | bytes 51714240 | solution.py:271
  983.9 136.8 %while.79 = (s32[]{:T(128)}, f32[512,8,64]{0,2,1:T(8,128)}, bf16[8,512,1024]{2,1,0:T(8,128)(2,1)}, bf16[8,512,8,64]{1,3,2,0:T(8,128)(2,1)}, s32[512]{0:T(512)S(1...) while((s32[]{:T(128)}, f32[512,8,64]{0,2,1:T(8,128)}, ...), condition=%wide.region_32.34_spmd.clone, body=%wide.region_31.33_spmd.clone.sunk | while | flops 1367353856 | bytes 51714240 | solution.py:271
  1155.3 125.2 %reduce-scatter.9.cloned.1.call-done = bf16[512,1024]{1,0:T(8,128)(2,1)} async-done(((bf16[4096,1024]{1,0:T(8,128)(2,1)}), bf16[512,1024]{1,0:T(8,128)(2,1)}) %reduce-scatter.9.cloned.1.call-update) | async-done | bytes 1048592 | tf_op jit(solution)/shard_map/reduce_scatter | solution.py:276
  1303.5 34.2 %reduce-scatter.15.cloned.1.call-done = bf16[128,2048]{1,0:T(8,128)(2,1)} async-done(((bf16[512,2048]{1,0:T(8,128)(2,1)}), bf16[128,2048]{1,0:T(8,128)(2,1)}) %reduce-scatter.15.cloned.1.call-update) | async-done | bytes 524304 | tf_op jit(solution)/shard_map/reduce_scatter | solution.py:302
  1337.7 34.0 %reduce-scatter.17.cloned.1.call-done = bf16[512,512]{1,0:T(8,128)(2,1)} async-done(((bf16[2048,512]{1,0:T(8,128)(2,1)}), bf16[512,512]{1,0:T(8,128)(2,1)}) %reduce-scatter.17.cloned.1.call-update) | async-done | bytes 524304 | tf_op jit(solution)/shard_map/reduce_scatter | solution.py:305
  1371.7 31.5 %reduce-scatter.11.cloned.1.call-done = bf16[128,1536]{1,0:T(8,128)(2,1)} async-done(((bf16[512,1536]{1,0:T(8,128)(2,1)}), bf16[128,1536]{1,0:T(8,128)(2,1)}) %reduce-scatter.11.cloned.1.call-update) | async-done | bytes 393232 | tf_op jit(solution)/shard_map/reduce_scatter | solution.py:296
  1419.5 22.0 %all-reduce.7 = (bf16[128]{0:T(256)(128)(2,1)S(1)}, bf16[128]{0:T(256)(128)(2,1)S(1)}, bf16[128]{0:T(256)(128)(2,1)S(1)}, bf16[128]{0:T(256)(128)(2,1)S(1)}, bf1...) all-reduce(bf16[128]{0:T(256)(128)(2,1)S(1)} %dynamic-slice.1, ...), channel_id=1, replica_groups=mesh['ctx'=8,'fsdp'=4] {'ctx'}, use_global_device_ids=true, to_apply=%region_47.49 | all-reduce | flops 1280 | bytes 5120 | tf_op jit(solution)/shard_map/psum | solution.py:335
  1448.4 48.8 %all-reduce.12.cloned.1.call-done = (bf16[128,1536]{1,0:T(8,128)(2,1)}, bf16[128,512]{1,0:T(8,128)(2,1)}, bf16[128,2048]{1,0:T(8,128)(2,1)}, bf16[512,512]{1,0:T(8,128)(2,1)}) async-done(((bf16[128,1536]{1,0:T(8,128)(2,1)}, bf16[128,512]{1,0:T(8,128)(2,1)}, bf16[128,2048]{1,0:T(8,128)(2,1)}, bf16[512,512]{1,0:T(8,128)(2,1)}), (bf16[128,1536]{1,0:T(8,128)(2,1)}, bf16[128,512]{1,0:T(8,128)(2,1)}, ...) | async-done | bytes 1572880 | tf_op jit(solution)/shard_map/psum | solution.py:331
  (860 shorter events, 801.2 us)
Async XLA Ops:
  7.2 24.8 %all-gather.13.cloned.1.call-start = ((), (), s32[]{:S(2)}) async-start(), calls=%async_computation.6 | async-start | bytes 1966080 | tf_op jit(solution)/shard_map/all_gather | solution.py:147
  7.9 652.6 %all-gather.15.cloned.1.call-start = ((), (), s32[]{:S(2)}) async-start(), calls=%async_computation.7 | async-start | bytes 2621440 | tf_op jit(solution)/shard_map/all_gather | solution.py:149
  8.7 657.4 %all-gather.17.cloned.1.call-start = ((), (), s32[]{:S(2)}) async-start(), calls=%async_computation.8 | async-start | bytes 2621440 | tf_op jit(solution)/shard_map/all_gather | solution.py:150
  34.8 28.8 %collective-permute-start = (bf16[512,1024]{1,0:T(8,128)(2,1)S(1)}, bf16[512,1024]{1,0:T(8,128)(2,1)}, u32[]{:S(2)}, u32[]{:S(2)}) collective-permute-start(bf16[512,1024]{1,0:T(8,128)(2,1)S(1)} %slice.84), channel_id=1, source_target_pairs={{0,4},{4,8},{8,12},{12,16},{16,20},{20,24},{24,28},{28,0},{1,5},{5... | collective-permute-start | bytes 3145736 | tf_op jit(solution)/shard_map/ppermute | solution.py:20
  39.7 87.6 %collective-permute-start.7 = (bf16[512,1024]{1,0:T(8,128)(2,1)}, bf16[512,1024]{1,0:T(8,128)(2,1)}, u32[]{:S(2)}, u32[]{:S(2)}) collective-permute-start(bf16[512,1024]{1,0:T(8,128)(2,1)} %slice.88), channel_id=1, source_target_pairs={{0,4},{4,8},{8,12},{12,16},{16,20},{20,24},{24,28},{28,0},{1,5},{5... | collective-permute-start | bytes 3145736 | tf_op jit(solution)/shard_map/ppermute | solution.py:20
  63.7 86.2 %collective-permute-start.1 = (bf16[512,1024]{1,0:T(8,128)(2,1)}, bf16[512,1024]{1,0:T(8,128)(2,1)}, u32[]{:S(2)}, u32[]{:S(2)}) collective-permute-start(bf16[512,1024]{1,0:T(8,128)(2,1)} %collective-permute-done), channel_id=1, source_target_pairs={{0,4},{4,8},{8,12},{12,16},{16,20},{20,24},{24,28},{28,0},{1,5},{5... | collective-permute-start | bytes 3145736 | tf_op jit(solution)/shard_map/ppermute | solution.py:20
  63.7 1087.4 %reduce-scatter.7.cloned.1.call-start = ((), (), s32[]{:S(2)}) async-start(), calls=%async_computation.9 | async-start | bytes 9437184 | tf_op jit(solution)/shard_map/reduce_scatter | solution.py:276
  75.2 77.9 %collective-permute-start.11 = (bf16[512,1024]{1,0:T(8,128)(2,1)}, bf16[512,1024]{1,0:T(8,128)(2,1)}, u32[]{:S(2)}, u32[]{:S(2)}) collective-permute-start(bf16[512,1024]{1,0:T(8,128)(2,1)} %slice.88), channel_id=1, source_target_pairs={{0,28},{4,0},{8,4},{12,8},{16,12},{20,16},{24,20},{28,24},{1,29},{... | collective-permute-start | bytes 3145736 | tf_op jit(solution)/shard_map/ppermute | solution.py:22
  79.9 118.0 %collective-permute-start.4 = (bf16[512,1024]{1,0:T(8,128)(2,1)}, bf16[512,1024]{1,0:T(8,128)(2,1)}, u32[]{:S(2)}, u32[]{:S(2)}) collective-permute-start(bf16[512,1024]{1,0:T(8,128)(2,1)} %copy-done.47), channel_id=1, source_target_pairs={{0,28},{4,0},{8,4},{12,8},{16,12},{20,16},{24,20},{28,24},{1,29},{... | collective-permute-start | bytes 3145736 | tf_op jit(solution)/shard_map/ppermute | solution.py:22
  127.4 71.0 %collective-permute-start.8 = (bf16[512,1024]{1,0:T(8,128)(2,1)}, bf16[512,1024]{1,0:T(8,128)(2,1)}, u32[]{:S(2)}, u32[]{:S(2)}) collective-permute-start(bf16[512,1024]{1,0:T(8,128)(2,1)} %collective-permute-done.7), channel_id=1, source_target_pairs={{0,4},{4,8},{8,12},{12,16},{16,20},{20,24},{24,28},{28,0},{1,5},{5... | collective-permute-start | bytes 3145736 | tf_op jit(solution)/shard_map/ppermute | solution.py:20
  149.8 89.9 %collective-permute-start.2 = (bf16[512,1024]{1,0:T(8,128)(2,1)}, bf16[512,1024]{1,0:T(8,128)(2,1)}, u32[]{:S(2)}, u32[]{:S(2)}) collective-permute-start(bf16[512,1024]{1,0:T(8,128)(2,1)} %collective-permute-done.1), channel_id=1, source_target_pairs={{0,4},{4,8},{8,12},{12,16},{16,20},{20,24},{24,28},{28,0},{1,5},{5... | collective-permute-start | bytes 3145736 | tf_op jit(solution)/shard_map/ppermute | solution.py:20
  153.0 268.6 %collective-permute-start.12 = (bf16[512,1024]{1,0:T(8,128)(2,1)}, bf16[512,1024]{1,0:T(8,128)(2,1)}, u32[]{:S(2)}, u32[]{:S(2)}) collective-permute-start(bf16[512,1024]{1,0:T(8,128)(2,1)} %collective-permute-done.11), channel_id=1, source_target_pairs={{0,28},{4,0},{8,4},{12,8},{16,12},{20,16},{24,20},{28,24},{1,29},{... | collective-permute-start | bytes 3145736 | tf_op jit(solution)/shard_map/ppermute | solution.py:22
  197.9 223.8 %collective-permute-start.5 = (bf16[512,1024]{1,0:T(8,128)(2,1)}, bf16[512,1024]{1,0:T(8,128)(2,1)}, u32[]{:S(2)}, u32[]{:S(2)}) collective-permute-start(bf16[512,1024]{1,0:T(8,128)(2,1)} %collective-permute-done.4), channel_id=1, source_target_pairs={{0,28},{4,0},{8,4},{12,8},{16,12},{20,16},{24,20},{28,24},{1,29},{... | collective-permute-start | bytes 3145736 | tf_op jit(solution)/shard_map/ppermute | solution.py:22
  198.4 224.3 %collective-permute-start.9 = (bf16[512,1024]{1,0:T(8,128)(2,1)}, bf16[512,1024]{1,0:T(8,128)(2,1)}, u32[]{:S(2)}, u32[]{:S(2)}) collective-permute-start(bf16[512,1024]{1,0:T(8,128)(2,1)} %collective-permute-done.8), channel_id=1, source_target_pairs={{0,4},{4,8},{8,12},{12,16},{16,20},{20,24},{24,28},{28,0},{1,5},{5... | collective-permute-start | bytes 3145736 | tf_op jit(solution)/shard_map/ppermute | solution.py:20
  239.7 184.2 %collective-permute-start.3 = (bf16[512,1024]{1,0:T(8,128)(2,1)}, bf16[512,1024]{1,0:T(8,128)(2,1)}, u32[]{:S(2)}, u32[]{:S(2)}) collective-permute-start(bf16[512,1024]{1,0:T(8,128)(2,1)} %collective-permute-done.2), channel_id=1, source_target_pairs={{0,4},{4,8},{8,12},{12,16},{16,20},{20,24},{24,28},{28,0},{1,5},{5... | collective-permute-start | bytes 3145736 | tf_op jit(solution)/shard_map/ppermute | solution.py:20
  421.6 75.0 %collective-permute-start.13 = (bf16[512,1024]{1,0:T(8,128)(2,1)}, bf16[512,1024]{1,0:T(8,128)(2,1)S(1)}, u32[]{:S(2)}, u32[]{:S(2)}) collective-permute-start(bf16[512,1024]{1,0:T(8,128)(2,1)} %collective-permute-done.12), channel_id=1, source_target_pairs={{0,28},{4,0},{8,4},{12,8},{16,12},{20,16},{24,20},{28,24},{1,29},{... | collective-permute-start | bytes 3145736 | tf_op jit(solution)/shard_map/ppermute | solution.py:22
  421.7 74.8 %collective-permute-start.6 = (bf16[512,1024]{1,0:T(8,128)(2,1)}, bf16[512,1024]{1,0:T(8,128)(2,1)S(1)}, u32[]{:S(2)}, u32[]{:S(2)}) collective-permute-start(bf16[512,1024]{1,0:T(8,128)(2,1)} %collective-permute-done.5), channel_id=1, source_target_pairs={{0,28},{4,0},{8,4},{12,8},{16,12},{20,16},{24,20},{28,24},{1,29},{... | collective-permute-start | bytes 3145736 | tf_op jit(solution)/shard_map/ppermute | solution.py:22
  422.7 67.1 %collective-permute-start.10 = (bf16[512,1024]{1,0:T(8,128)(2,1)}, bf16[512,1024]{1,0:T(8,128)(2,1)S(1)}, u32[]{:S(2)}, u32[]{:S(2)}) collective-permute-start(bf16[512,1024]{1,0:T(8,128)(2,1)} %collective-permute-done.9), channel_id=1, source_target_pairs={{0,4},{4,8},{8,12},{12,16},{16,20},{20,24},{24,28},{28,0},{1,5},{5... | collective-permute-start | bytes 3145736 | tf_op jit(solution)/shard_map/ppermute | solution.py:20
  979.1 301.4 %reduce-scatter.9.cloned.1.call-start = ((), (), s32[]{:S(2)}) async-start(), calls=%async_computation.10 | async-start | bytes 9437184 | tf_op jit(solution)/shard_map/reduce_scatter | solution.py:276
  1120.8 182.7 %reduce-scatter.13.cloned.1.call-start = ((), (), s32[]{:S(2)}) async-start(), calls=%async_computation.12 | async-start | bytes 655360 | tf_op jit(solution)/shard_map/reduce_scatter | solution.py:299
  1123.7 213.9 %reduce-scatter.15.cloned.1.call-start = ((), (), s32[]{:S(2)}) async-start(), calls=%async_computation.13 | async-start | bytes 2621440 | tf_op jit(solution)/shard_map/reduce_scatter | solution.py:302
  1129.7 241.9 %reduce-scatter.17.cloned.1.call-start = ((), (), s32[]{:S(2)}) async-start(), calls=%async_computation.14 | async-start | bytes 2621440 | tf_op jit(solution)/shard_map/reduce_scatter | solution.py:305
  1135.9 267.3 %reduce-scatter.11.cloned.1.call-start = ((), (), s32[]{:S(2)}) async-start(), calls=%async_computation.11 | async-start | bytes 1966080 | tf_op jit(solution)/shard_map/reduce_scatter | solution.py:296
  1284.9 212.2 %all-reduce.12.cloned.1.call-start = ((), (), s32[]{:S(2)}) async-start(), calls=%async_computation.15 | async-start | bytes 3145728 | tf_op jit(solution)/shard_map/psum | solution.py:331
  (106 other events, 4223.2 us)
Sparse Core Ops, SparseCore 0:
  9.6 22.3 all-gather.12
  33.5 22.5 all-gather.14
  63.8 23.0 all-gather.16
  979.2 149.3 reduce-scatter.6
  1132.5 147.9 reduce-scatter.8
  1282.8 20.6 reduce-scatter.12
  1306.2 31.4 reduce-scatter.14
  1340.2 31.4 reduce-scatter.16
  1375.0 28.1 reduce-scatter.10
  1406.8 90.2 all-reduce.11
